TPU v7x, 32 devices: a whole 2x2x4 slice. The times are simulated.
32 devices in a mesh: dp: 8 (over z, core), tensor: 4 (over y, x).
Axes of the slice: x: 2, y: 2, z: 4, core: 2. Of those that a mesh axis runs over, the one named last changes fastest.
Arguments:
- inputs: bfloat16 [8, 1024, 1024], P('dp'), may hold values from -6 to 6
- cotangent: bfloat16 [8, 1024, 1024], P('dp'), may hold values from -6 to 6
- groups: int32 [8], P('dp'), may hold values from 0 to 7
- counts: int32 [8], replicated, may hold values from 128 to 512
- vector_parameters: float32 [6, 1024], replicated, may hold values from -0.9 to 1.4, as said below
- query_value_bias: float32 [2, 1024], P(None, 'tensor'), may hold values from -1.8 to 1.8
- hidden_bias: float32 [4096], P('tensor'), may hold values from -1.8 to 1.8
- query_key_value_weight: bfloat16 [3, 1024, 1024], P(None, None, 'tensor'), may hold values from -0.1875 to 0.1875
- attention_output_weight: bfloat16 [1024, 1024], P('tensor'), may hold values from -0.75 to 0.75
- hidden_weight: bfloat16 [1024, 4096], P(None, 'tensor'), may hold values from -0.1875 to 0.1875
- hidden_output_weight: bfloat16 [4096, 1024], P('tensor'), may hold values from -0.09375 to 0.09375
- adapter_down: float32 [2, 1024, 4], replicated, may hold values from -0.1875 to 0.1875
- adapter_up: float32 [2, 4, 1024], replicated, may hold values from -0.18 to 0.18
- momentum_down: float32 [2, 1024, 4], replicated, may hold values from -0.039774757 to 0.039774757
- momentum_up: float32 [2, 4, 1024], replicated, may hold values from -0.079549514 to 0.079549514
- average_down: float32 [2, 1024, 4], replicated, may hold values from -0.1875 to 0.1875
- average_up: float32 [2, 4, 1024], replicated, may hold values from -0.18 to 0.18
Outputs:
- block_out: bfloat16 [8, 1024, 1024], P('dp')
- input_grad: bfloat16 [8, 1024, 1024], P('dp')
- down_gradient: float32 [2, 1024, 4], replicated
- up_gradient: float32 [2, 4, 1024], replicated
- updated_momentum_down: float32 [2, 1024, 4], replicated
- updated_momentum_up: float32 [2, 4, 1024], replicated
- updated_down: float32 [2, 1024, 4], replicated
- updated_up: float32 [2, 4, 1024], replicated
- updated_average_down: float32 [2, 1024, 4], replicated
- updated_average_up: float32 [2, 4, 1024], replicated
- copy_a: bfloat16 [2, 1024, 4], replicated
- copy_b: bfloat16 [2, 4, 1024], replicated
Inputs may be any that keep to these rules, and one draw needn't show every extreme that they name: `vector_parameters`: rows 0 and 2 are gains, the other rows shifts and biases.
All inputs are finite; a program needn't handle non-finite values.
Results may differ from a plain program's by a relative error of at most 0.018.
Values may be sent and summed in bfloat16 or wider, within the bound.
No kernel may reach another device: no remote copies, remote signals or barrier semaphores. Data moves between devices by JAX's collectives and lax.ppermute only.
A program may use at most 128 MiB of HBM per device.

v0:
```python
import math
import jax
import jax.numpy as jnp
from jax import lax
from jax.sharding import PartitionSpec as P

HEAD = 64
NORM_EPS = 1e-05
ADAPTER_SCALE = 8.0
MASK_FILL = -1e30
MOMENTUM_FACTOR = 0.9
AVERAGE_KEEP = 0.8
RATE_BASE = 0.025
WEIGHT_DECAY = 0.005
COUNT_BASE = 256.0


def layer_norm(value_rows, norm_gain, norm_bias):
    center = value_rows - jnp.mean(value_rows, axis=-1, keepdims=True)
    spread = jnp.mean(center * center, axis=-1, keepdims=True)
    return center * lax.rsqrt(spread + NORM_EPS) * norm_gain + norm_bias


def norm_back(value_rows, norm_gain, norm_bias, upstream):

    def local_norm(operand):
        return layer_norm(operand, norm_gain, norm_bias)

    _, backward_map = jax.vjp(local_norm, value_rows)
    return backward_map(upstream)[0]


def gelu_back(preact, upstream):

    def activate(operand):
        return jax.nn.gelu(operand, approximate=True)

    _, backward_map = jax.vjp(activate, preact)
    return backward_map(upstream)[0]


def to_heads(matrix, seq_count, length):
    return matrix.reshape(seq_count, length, -1, HEAD).transpose(0, 2, 1, 3)


def to_rows(tensor4):
    return tensor4.transpose(0, 2, 1, 3).reshape(-1, tensor4.shape[1] * tensor4.shape[3])


def block_scores(query_block, keys, offset, scale_att):
    scores = (
        jnp.einsum("shqe,shke->shqk", query_block, keys, preferred_element_type=jnp.float32)
        * scale_att
    )
    query_pos = offset + jnp.arange(query_block.shape[2])
    key_pos = jnp.arange(keys.shape[2])
    return jnp.where(key_pos[None, :] <= query_pos[:, None], scores, MASK_FILL)


def attend(query_rows, keys, value_rows, scale_att):
    length = query_rows.shape[2]
    block_len = min(512, length)
    outputs = []
    log_totals = []
    for offset in range(0, length, block_len):
        query_block = query_rows[:, :, offset : offset + block_len]
        scores = block_scores(query_block, keys, offset, scale_att)
        largest = jnp.max(scores, axis=-1, keepdims=True)
        exponent = jnp.exp(scores - largest)
        summed = jnp.sum(exponent, axis=-1, keepdims=True)
        attention = exponent / summed
        log_totals.append(largest + jnp.log(summed))
        outputs.append(
            jnp.einsum(
                "shqk,shke->shqe",
                attention.astype(jnp.bfloat16),
                value_rows,
                preferred_element_type=jnp.float32,
            )
        )
    return (jnp.concatenate(outputs, axis=2), log_totals)


def attend_back(query_rows, keys, value_rows, log_totals, grad_heads, scale_att):
    length = query_rows.shape[2]
    block_len = min(512, length)
    grad_blocks = []
    grad_keys = jnp.zeros(keys.shape, jnp.float32)
    grad_values = jnp.zeros(value_rows.shape, jnp.float32)
    for number, offset in enumerate(range(0, length, block_len)):
        query_block = query_rows[:, :, offset : offset + block_len]
        grad_block = grad_heads[:, :, offset : offset + block_len]
        scores = block_scores(query_block, keys, offset, scale_att)
        attention = jnp.exp(scores - log_totals[number])
        grad_attn = jnp.einsum(
            "shqe,shke->shqk", grad_block, value_rows, preferred_element_type=jnp.float32
        )
        row_inner = jnp.sum(grad_attn * attention, axis=-1, keepdims=True)
        grad_scores = (attention * (grad_attn - row_inner)).astype(jnp.bfloat16)
        grad_blocks.append(
            jnp.einsum("shqk,shke->shqe", grad_scores, keys, preferred_element_type=jnp.float32)
            * scale_att
        )
        grad_keys = (
            grad_keys
            + jnp.einsum(
                "shqk,shqe->shke", grad_scores, query_block, preferred_element_type=jnp.float32
            )
            * scale_att
        )
        grad_values = grad_values + jnp.einsum(
            "shqk,shqe->shke",
            attention.astype(jnp.bfloat16),
            grad_block,
            preferred_element_type=jnp.float32,
        )
    return (jnp.concatenate(grad_blocks, axis=2), grad_keys, grad_values)


def update_step(gradient_term, moment, weight_matrix, average, learning_rate):
    updated_moment = MOMENTUM_FACTOR * moment + gradient_term
    updated_weight = weight_matrix * (
        1.0 - learning_rate * WEIGHT_DECAY * ADAPTER_SCALE
    ) - learning_rate * (gradient_term + MOMENTUM_FACTOR * updated_moment)
    new_average = AVERAGE_KEEP * average + (1.0 - AVERAGE_KEEP) * updated_weight
    return (updated_moment, updated_weight, new_average)


def local(
    inputs,
    cotangent,
    groups,
    counts,
    vector_parameters,
    query_value_bias,
    hidden_bias,
    query_key_value_weight,
    attention_output_weight,
    hidden_weight,
    hidden_output_weight,
    adapter_down,
    adapter_up,
    momentum_down,
    momentum_up,
    average_down,
    average_up,
):
    seq_count, length, width_value = inputs.shape
    row_count = seq_count * length
    resid_in = inputs.reshape(row_count, width_value).astype(jnp.float32)
    first_norm_output = layer_norm(resid_in, vector_parameters[0], vector_parameters[1]).astype(
        jnp.bfloat16
    )
    local_width = query_key_value_weight.shape[2]
    column_start = lax.axis_index("tensor") * local_width
    down_reduced = adapter_down.astype(jnp.bfloat16)
    up_reduced = adapter_up.astype(jnp.bfloat16)
    up_local = lax.dynamic_slice_in_dim(up_reduced, column_start, local_width, 2)
    projected_rows = jnp.einsum(
        "rd,cde->cre", first_norm_output, query_key_value_weight, preferred_element_type=jnp.float32
    )
    adapter_input = jnp.einsum(
        "wo,qob->qwb", first_norm_output, down_reduced, preferred_element_type=jnp.float32
    ).astype(jnp.bfloat16)
    adapter_output = jnp.einsum(
        "iga,iaj->igj", adapter_input, up_local, preferred_element_type=jnp.float32
    )
    query_rows = (
        projected_rows[0] + query_value_bias[0] + ADAPTER_SCALE * adapter_output[0]
    ).astype(jnp.bfloat16)
    keys_low = projected_rows[1].astype(jnp.bfloat16)
    value_reduced = (
        projected_rows[2] + query_value_bias[1] + ADAPTER_SCALE * adapter_output[1]
    ).astype(jnp.bfloat16)
    scale_att = HEAD ** (-0.5)
    query_heads = to_heads(query_rows, seq_count, length)
    key_heads = to_heads(keys_low, seq_count, length)
    value_heads = to_heads(value_reduced, seq_count, length)
    heads_out, log_totals = attend(query_heads, key_heads, value_heads, scale_att)
    merged = to_rows(heads_out).astype(jnp.bfloat16)
    attn_part = jnp.dot(merged, attention_output_weight, preferred_element_type=jnp.float32)
    tile = row_count // lax.axis_size("tensor")
    row_offset = lax.axis_index("tensor") * tile
    one_hot = groups[:, None] == jnp.arange(counts.shape[0])[None, :]
    seq_counts = jnp.sum(jnp.where(one_hot, counts[None, :], 0), axis=1).astype(jnp.float32)
    seq_weight = COUNT_BASE / seq_counts
    grad_out = (cotangent.astype(jnp.float32) * seq_weight[:, None, None]).reshape(
        row_count, width_value
    )
    grad_low = grad_out.astype(jnp.bfloat16)
    attn_share = lax.psum_scatter(
        attn_part.astype(jnp.bfloat16), "tensor", scatter_dimension=0, tiled=True
    ).astype(jnp.float32)
    input_share = lax.dynamic_slice_in_dim(resid_in, row_offset, tile, 0)
    resid_share = input_share + attn_share + vector_parameters[4]
    norm_share = layer_norm(resid_share, vector_parameters[2], vector_parameters[3]).astype(
        jnp.bfloat16
    )
    norm2 = lax.all_gather(norm_share, "tensor", axis=0, tiled=True)
    preact = jnp.dot(norm2, hidden_weight, preferred_element_type=jnp.float32) + hidden_bias
    act_low = jax.nn.gelu(preact, approximate=True).astype(jnp.bfloat16)
    preact, mlp_part = (
        preact,
        jnp.dot(act_low, hidden_output_weight, preferred_element_type=jnp.float32),
    )
    mlp_share = lax.psum_scatter(
        mlp_part.astype(jnp.bfloat16), "tensor", scatter_dimension=0, tiled=True
    ).astype(jnp.float32)
    output_share = (resid_share + mlp_share + vector_parameters[5]).astype(jnp.bfloat16)
    output_rows = lax.all_gather(output_share, "tensor", axis=0, tiled=True)
    grad_act = jnp.einsum(
        "rd,fd->rf", grad_low, hidden_output_weight, preferred_element_type=jnp.float32
    )
    grad_pre = gelu_back(preact, grad_act).astype(jnp.bfloat16)
    grad_norm_share = lax.psum_scatter(
        jnp.einsum("rf,df->rd", grad_pre, hidden_weight, preferred_element_type=jnp.float32).astype(
            jnp.bfloat16
        ),
        "tensor",
        scatter_dimension=0,
        tiled=True,
    ).astype(jnp.float32)
    grad_out_share = lax.dynamic_slice_in_dim(grad_out, row_offset, tile, 0)
    grad_resid_share = grad_out_share + norm_back(
        resid_share, vector_parameters[2], vector_parameters[3], grad_norm_share
    )
    grad_resid_low = lax.all_gather(
        grad_resid_share.astype(jnp.bfloat16), "tensor", axis=0, tiled=True
    )
    grad_merged = jnp.einsum(
        "rd,ed->re", grad_resid_low, attention_output_weight, preferred_element_type=jnp.float32
    ).astype(jnp.bfloat16)
    grad_q, grad_k, grad_v = attend_back(
        query_heads,
        key_heads,
        value_heads,
        log_totals,
        to_heads(grad_merged, seq_count, length),
        scale_att,
    )
    grad_qkv = jnp.stack([to_rows(grad_q), to_rows(grad_k), to_rows(grad_v)]).astype(jnp.bfloat16)
    grad_norm1 = jnp.einsum(
        "cre,cde->rd", grad_qkv, query_key_value_weight, preferred_element_type=jnp.float32
    )
    query_value_gradient = jnp.stack([grad_qkv[0], grad_qkv[2]])
    adapter_input_gradient = ADAPTER_SCALE * jnp.einsum(
        "cre,cke->crk", query_value_gradient, up_local, preferred_element_type=jnp.float32
    )
    grad_norm1 = grad_norm1 + jnp.einsum(
        "ibp,inp->bn",
        adapter_input_gradient,
        down_reduced.astype(jnp.float32),
        precision=lax.Precision.HIGHEST,
    )
    grad_a_part = jnp.einsum(
        "rd,crk->cdk",
        first_norm_output,
        adapter_input_gradient,
        precision=lax.Precision.HIGHEST,
        preferred_element_type=jnp.float32,
    )
    local_up_gradient = ADAPTER_SCALE * jnp.einsum(
        "ipg,ipd->igd", adapter_input, query_value_gradient, preferred_element_type=jnp.float32
    )
    grad_b_part = lax.dynamic_update_slice(
        jnp.zeros((2, adapter_up.shape[1], width_value), jnp.float32),
        local_up_gradient,
        (0, 0, column_start),
    )
    grad_norm1_share = lax.psum_scatter(
        grad_norm1.astype(jnp.bfloat16), "tensor", scatter_dimension=0, tiled=True
    ).astype(jnp.float32)
    grad_input_share = grad_resid_share + norm_back(
        input_share, vector_parameters[0], vector_parameters[1], grad_norm1_share
    )
    grad_a_sum, grad_b_sum, weight_sum = lax.psum(
        (grad_a_part, grad_b_part, jnp.sum(seq_weight)), ("dp", "tensor")
    )
    mean_weight = weight_sum / (lax.axis_size("dp") * lax.axis_size("tensor") * seq_count)
    tokens_all = lax.axis_size("dp") * seq_count * length
    input_grad = lax.all_gather(
        (grad_input_share / mean_weight).astype(jnp.bfloat16), "tensor", axis=0, tiled=True
    )
    down_gradient = grad_a_sum / (mean_weight * tokens_all)
    up_gradient = grad_b_sum / (mean_weight * tokens_all)
    learning_rate = RATE_BASE * math.sqrt(tokens_all)
    updated_momentum_down, updated_down, updated_average_down = update_step(
        down_gradient, momentum_down, adapter_down, average_down, learning_rate
    )
    updated_momentum_up, updated_up, updated_average_up = update_step(
        up_gradient, momentum_up, adapter_up, average_up, learning_rate
    )
    block_out = output_rows.reshape(seq_count, length, width_value)
    input_grad = input_grad.reshape(seq_count, length, width_value)
    return (
        block_out,
        input_grad,
        down_gradient,
        up_gradient,
        updated_momentum_down,
        updated_momentum_up,
        updated_down,
        updated_up,
        updated_average_down,
        updated_average_up,
        updated_down.astype(jnp.bfloat16),
        updated_up.astype(jnp.bfloat16),
    )


def solution(mesh):
    in_specs = (
        P("dp", None, None),
        P("dp", None, None),
        P("dp"),
        P(),
        P(),
        P(None, "tensor"),
        P("tensor"),
        P(None, None, "tensor"),
        P("tensor", None),
        P(None, "tensor"),
        P("tensor", None),
        P(),
        P(),
        P(),
        P(),
        P(),
        P(),
    )
    out_specs = (
        P("dp", None, None),
        P("dp", None, None),
        P(),
        P(),
        P(),
        P(),
        P(),
        P(),
        P(),
        P(),
        P(),
        P(),
    )
    return jax.shard_map(local, mesh=mesh, in_specs=in_specs, out_specs=out_specs, check_vma=False)
```

profile of v0, /device:TPU:0, one launch (start us, length us, event | category | flops | bytes accessed | tf_op | source)
XLA Modules:
  0.0 417.0 jit_solution(1746353176748242203)
XLA Ops:
  11.2 2.3 multiply_reduce_fusion.2
  13.5 2.4 fusion.20
  20.3 3.0 fusion.93
  26.9 2.2 reshape.355
  31.4 3.2 fusion.94
  34.6 1.9 fusion.95
  44.5 2.1 convolution_convert_fusion.1
  46.6 4.0 convert_element_type.147
  50.6 34.0 %reduce-scatter.5.cloned.1.call-done = bf16[256,1024]{1,0:T(8,128)(2,1)} async-done(((bf16[1024,1024]{1,0:T(8,128)(2,1)}), bf16[256,1024]{1,0:T(8,128)(2,1)}) %reduce-scatter.5.cloned.1.call-update) | async-done | bytes 524304 | tf_op jit(solution)/shard_map/reduce_scatter | solution.py:191
  89.6 33.3 %all-gather.5.cloned.1.call-done = bf16[1024,1024]{1,0:T(8,128)(2,1)} async-done(((bf16[256,1024]{1,0:T(8,128)(2,1)}), bf16[1024,1024]{1,0:T(8,128)(2,1)}) %all-gather.5.cloned.1.call-update) | async-done | bytes 2097168 | tf_op jit(solution)/shard_map/all_gather | solution.py:199
  122.9 5.9 %fusion.96 = f32[1024,1024]{1,0:T(8,128)} fusion(bf16[1024,1024]{1,0:T(8,128)(2,1)} %all-gather.5.cloned.1.call-done, bf16[1024,1024]{1,0:T(8,128)(2,1)S(1)} %copy-done), kind=kOutput, calls=%fused_computation.171 | convolution fusion | flops 2147483648 | bytes 8388608 | tf_op jit(solution)/shard_map/dot_general | solution.py:200
  128.8 9.5 %convolution_convert_fusion = bf16[1024,1024]{1,0:T(8,128)(2,1)} fusion(bf16[1024,1024]{1,0:T(8,128)(2,1)S(1)} %copy-done, f32[1024,1024]{1,0:T(8,128)} %fusion.96, bf16[1024,1024]{1,0:T(8,128)(2,1)} %param.27, f32[1024]{0:T(1024)S(1)} %copy-done.36, bf16[1,1024,1024]{2,1,0:T(8,128)(2,1)} %param.18, f32[]{:T(128)S(6)} %div.95), kind=kOutput, calls=%fused_computation.47 | convolution fusion | flops 4321181696 | bytes 12587012 | tf_op jit(solution)/shard_map/rf,df->rd/dot_general | solution.py:216
  138.3 7.1 %fusion.27 = bf16[1024,1024]{1,0:T(8,128)(2,1)} fusion(bf16[1024,1024]{1,0:T(8,128)(2,1)} %param.27, f32[1024,1024]{1,0:T(8,128)} %fusion.96, f32[1024]{0:T(1024)S(1)} %copy-done.36), kind=kOutput, calls=%fused_computation.46 | convolution fusion | flops 2159017984 | bytes 8392704 | tf_op jit(solution)/shard_map/dot_general | solution.py:204
  145.8 2.5 convert_multiply_fusion
  148.3 25.3 %reduce-scatter.9.cloned.1.call-done = bf16[256,1024]{1,0:T(8,128)(2,1)} async-done(((bf16[1024,1024]{1,0:T(8,128)(2,1)}), bf16[256,1024]{1,0:T(8,128)(2,1)}) %reduce-scatter.9.cloned.1.call-update) | async-done | bytes 524304 | tf_op jit(solution)/shard_map/reduce_scatter | solution.py:215
  174.9 36.7 %reduce-scatter.7.cloned.1.call-done = bf16[256,1024]{1,0:T(8,128)(2,1)} async-done(((bf16[1024,1024]{1,0:T(8,128)(2,1)}), bf16[256,1024]{1,0:T(8,128)(2,1)}) %reduce-scatter.7.cloned.1.call-update) | async-done | bytes 524304 | tf_op jit(solution)/shard_map/reduce_scatter | solution.py:206
  211.7 2.4 fusion.87
  214.1 2.6 fusion.63
  216.7 35.2 %all-gather.9.cloned.1.call-done = bf16[1024,1024]{1,0:T(8,128)(2,1)} async-done(((bf16[256,1024]{1,0:T(8,128)(2,1)}), bf16[1024,1024]{1,0:T(8,128)(2,1)}) %all-gather.9.cloned.1.call-update) | async-done | bytes 2097168 | tf_op jit(solution)/shard_map/all_gather | solution.py:227
  252.0 2.5 convolution_convert_fusion.2
  254.5 5.0 %fusion.11 = f32[4,1024,64]{1,2,0:T(8,128)S(1)} fusion(f32[4,512,1024]{2,1,0:T(8,128)} %copy-done.2, f32[4,512]{1,0:T(4,128)S(1)} %log_add_fusion, bf16[1,4,1024,64]{2,3,1,0:T(8,128)(2,1)S(1)} %bitcast.159), kind=kOutput, calls=%fused_computation.25 | convolution fusion | flops 272629760 | bytes 9707520 | tf_op jit(solution)/shard_map/shqk,shqe->shke/dot_general | solution.py:111
  259.6 4.3 %multiply_reduce_fusion = (f32[4,512]{1,0:T(4,128)S(1)}, f32[4,512,1024]{2,1,0:T(8,128)}) fusion(f32[4,512,1024]{2,1,0:T(8,128)S(1)} %bitcast.151, f32[4,512]{1,0:T(4,128)S(1)} %log_add_fusion, bf16[4,1024,64]{1,2,0:T(8,128)(2,1)S(1)} %copy-done.12, bf16[1,4,1024,64]{2,3,1,0:T(8,128)(2,1)S(1)} %bitcast.160), kind=kOutput, calls=%fused_computation.1 | convolution fusion | flops 274724864 | bytes 17580032 | tf_op jit(solution)/shard_map/shqe,shke->shqk/dot_general | solution.py:95
  263.9 2.6 multiply_reduce_fusion.1
  272.5 6.9 %multiply_convert_fusion = bf16[4,512,1024]{2,1,0:T(8,128)(2,1)S(1)} fusion(f32[4,512,1024]{2,1,0:T(8,128)} %get-tuple-element.55, f32[4,512,1024]{2,1,0:T(8,128)} %copy-done.2, f32[4,512]{1,0:T(4,128)S(1)} %get-tuple-element.54, f32[4,512]{1,0:T(4,128)S(1)} %log_add_fusion), kind=kLoop, calls=%fused_computation | loop fusion | flops 8388608 | bytes 20987904 | tf_op jit(solution)/shard_map/convert_element_type | solution.py:99
  279.5 1.9 copy-done.4
  283.5 3.8 fusion.64
  288.5 5.8 %fusion.15 = bf16[1024,1024]{1,0:T(8,128)(2,1)} fusion(f32[1024,1024,1]{1,0,2:T(8,128)} %fusion.64, bf16[3,1024,256]{2,1,0:T(8,128)(2,1)} %param.24, bf16[1,1024,256]{2,1,0:T(8,128)(2,1)S(1)} %copy.36, bf16[1,1024,256]{2,1,0:T(8,128)(2,1)S(1)} %copy.35, bf16[1,1024,256]{2,1,0:T(8,128)(2,1)S(1)} %copy.34), kind=kOutput, calls=%fused_computation.28 | convolution fusion | flops 1614282752 | bytes 9437184 | tf_op jit(solution)/shard_map/cre,cde->rd/dot_general | solution.py:242
  299.3 40.8 %all-reduce.2 = (f32[]{:T(128)}, f32[2,1024,4]{1,2,0:T(4,128)S(1)}, f32[2,4,1024]{2,1,0:T(4,128)S(1)}) all-reduce(f32[]{:T(128)S(6)} %div.95, f32[2,1024,4]{1,2,0:T(4,128)S(1)} %convolution_bitcast_fusion.1, f32[2,4,1024]{2,1,0:T(4,128)S(1)} %fusion.52), channel_id=1, replica_groups=mesh['dp'=8,'tensor'=4] {'dp','tensor'}, use_global_device_ids=true, to_apply=%region_21.22 | all-reduce | flops 16385 | bytes 131080 | tf_op jit(solution)/shard_map/psum | solution.py:276
  344.3 3.0 divide_convert_fusion.12
  348.0 19.5 %all-gather.7.cloned.1.call-done = bf16[1024,1024]{1,0:T(8,128)(2,1)} async-done(((bf16[256,1024]{1,0:T(8,128)(2,1)}), bf16[1024,1024]{1,0:T(8,128)(2,1)}) %all-gather.7.cloned.1.call-update) | async-done | bytes 2097168 | tf_op jit(solution)/shard_map/all_gather | solution.py:210
  370.1 35.1 %all-gather.11.cloned.1.call-done = bf16[1024,1024]{1,0:T(8,128)(2,1)} async-done(((bf16[256,1024]{1,0:T(8,128)(2,1)}), bf16[1024,1024]{1,0:T(8,128)(2,1)}) %all-gather.11.cloned.1.call-update) | async-done | bytes 2097168 | tf_op jit(solution)/shard_map/all_gather | solution.py:281
  405.1 3.2 copy.59
  (161 shorter events, 48.9 us)
Async XLA Ops:
  7.2 115.7 %copy-start = (bf16[1024,1024]{1,0:T(8,128)(2,1)S(1)}, bf16[1024,1024]{1,0:T(8,128)(2,1)}, u32[]{:S(2)}) copy-start(bf16[1024,1024]{1,0:T(8,128)(2,1)} %param.26) | copy-start | bytes 6291460
  7.2 77.5 %reduce-scatter.5.cloned.1.call-start = ((), (), s32[]{:S(2)}) async-start(), calls=%async_computation.4 | async-start | bytes 2621440 | tf_op jit(solution)/shard_map/reduce_scatter | solution.py:191
  9.2 8.0 %copy-start.26 = (f32[2,1024,4]{1,2,0:T(4,128)S(1)}, f32[2,1024,4]{1,2,0:T(4,128)}, u32[]{:S(2)}) copy-start(f32[2,1024,4]{1,2,0:T(4,128)} %param.28) | copy-start | bytes 98308
  11.1 6.7 %copy-start.29 = (f32[2,4,1024]{2,1,0:T(4,128)S(1)}, f32[2,4,1024]{2,1,0:T(4,128)}, u32[]{:S(2)}) copy-start(f32[2,4,1024]{2,1,0:T(4,128)} %param.29) | copy-start | bytes 98308
  36.5 5.9 %copy-start.3 = (f32[4,512,1024]{2,1,0:T(8,128)}, f32[4,512,1024]{2,1,0:T(8,128)S(1)}, u32[]{:S(2)}) copy-start(f32[4,512,1024]{2,1,0:T(8,128)S(1)} %get-tuple-element.53) | copy-start | bytes 25165828
  46.6 76.3 %all-gather.5.cloned.1.call-start = ((), (), s32[]{:S(2)}) async-start(), calls=%async_computation.5 | async-start | bytes 2621440 | tf_op jit(solution)/shard_map/all_gather | solution.py:199
  50.6 37.7 %copy-start.37 = (s32[8]{0:T(128)S(1)}, s32[8]{0:T(128)}, u32[]{:S(2)}) copy-start(s32[8]{0:T(128)} %param.20) | copy-start | bytes 100
  87.6 86.0 %reduce-scatter.9.cloned.1.call-start = ((), (), s32[]{:S(2)}) async-start(), calls=%async_computation.8 | async-start | bytes 2621440 | tf_op jit(solution)/shard_map/reduce_scatter | solution.py:215
  89.6 39.2 %copy-start.36 = (f32[1024]{0:T(1024)S(1)}, f32[1024]{0:T(1024)}, u32[]{:S(2)}) copy-start(f32[1024]{0:T(1024)} %param.23) | copy-start | bytes 12292
  138.3 7.5 %copy-start.16 = (bf16[1,1024,1024]{2,1,0:T(8,128)(2,1)S(1)}, bf16[1,1024,1024]{2,1,0:T(8,128)(2,1)}, u32[]{:S(2)}) copy-start(bf16[1,1024,1024]{2,1,0:T(8,128)(2,1)} %param.18) | copy-start | bytes 6291460
  138.3 73.4 %reduce-scatter.7.cloned.1.call-start = ((), (), s32[]{:S(2)}) async-start(), calls=%async_computation.6 | async-start | bytes 2621440 | tf_op jit(solution)/shard_map/reduce_scatter | solution.py:206
  145.5 106.5 %all-gather.9.cloned.1.call-start = ((), (), s32[]{:S(2)}) async-start(), calls=%async_computation.9 | async-start | bytes 2621440 | tf_op jit(solution)/shard_map/all_gather | solution.py:227
  148.3 103.7 %copy-start.25 = (bf16[256,1024]{1,0:T(8,128)(2,1)S(1)}, bf16[256,1024]{1,0:T(8,128)(2,1)}, u32[]{:S(2)}) copy-start(bf16[256,1024]{1,0:T(8,128)(2,1)} %param.25) | copy-start | bytes 1572868
  214.1 40.4 %copy-start.9 = (f32[256,1024]{1,0:T(8,128)}, f32[256,1024]{1,0:T(8,128)S(1)}, u32[]{:S(2)}) copy-start(f32[256,1024]{1,0:T(8,128)S(1)} %get-tuple-element.28) | copy-start | bytes 3145732
  216.7 124.1 %reduce-scatter.11.cloned.1.call-start = ((), (), s32[]{:S(2)}) async-start(), calls=%async_computation.10 | async-start | bytes 2621440 | tf_op jit(solution)/shard_map/reduce_scatter | solution.py:270
  252.0 7.5 %slice-start = ((s8[8388608]{0:T(1024)(128)(4,1)}), s8[4194304]{0:T(1024)(128)(4,1)S(1)}, s32[]{:S(2)}) async-start(s8[8388608]{0:T(1024)(128)(4,1)} %bitcast.150), calls=%async_computation.12 | async-start | bytes 8388608
  254.5 5.0 %slice-start.1 = ((s8[8388608]{0:T(1024)(128)(4,1)}), s8[4194304]{0:T(1024)(128)(4,1)S(1)}, s32[]{:S(2)}) async-start(s8[8388608]{0:T(1024)(128)(4,1)} %bitcast.150), calls=%async_computation.13 | async-start | bytes 8388608
  254.5 5.0 %copy-start.12 = (bf16[4,1024,64]{1,2,0:T(8,128)(2,1)S(1)}, bf16[4,1024,64]{1,2,0:T(8,128)(2,1)}, u32[]{:S(2)}) copy-start(bf16[4,1024,64]{1,2,0:T(8,128)(2,1)} %copy-done.11) | copy-start | bytes 1572868
  254.5 9.4 %slice-start.2 = ((s8[8388608]{0:T(1024)(128)(4,1)}), s8[4194304]{0:T(1024)(128)(4,1)S(1)}, s32[]{:S(2)}) async-start(s8[8388608]{0:T(1024)(128)(4,1)} %bitcast.152), calls=%async_computation.14 | async-start | bytes 8388608
  272.5 16.0 %copy-start.22 = (bf16[1,1024,256]{2,1,0:T(8,128)(2,1)}, bf16[1,1024,256]{2,1,0:T(8,128)(2,1)S(1)}, u32[]{:S(2)}) copy-start(bf16[1,1024,256]{2,1,0:T(8,128)(2,1)S(1)} %copy.36) | copy-start | bytes 1572868
  272.5 8.9 %copy-start.20 = (bf16[4,1024,64]{1,0,2:T(4,128)(2,1)S(1)}, bf16[4,1024,64]{1,0,2:T(4,128)(2,1)}, u32[]{:S(2)}) copy-start(bf16[4,1024,64]{1,0,2:T(4,128)(2,1)} %reshape.355) | copy-start | bytes 1572868
  283.1 5.3 %copy-start.23 = (bf16[1,1024,256]{2,1,0:T(8,128)(2,1)}, bf16[1,1024,256]{2,1,0:T(8,128)(2,1)S(1)}, u32[]{:S(2)}) copy-start(bf16[1,1024,256]{2,1,0:T(8,128)(2,1)S(1)} %copy.34) | copy-start | bytes 1572868
  294.3 73.2 %all-gather.7.cloned.1.call-start = ((), (), s32[]{:S(2)}) async-start(), calls=%async_computation.7 | async-start | bytes 2621440 | tf_op jit(solution)/shard_map/all_gather | solution.py:210
  294.4 49.9 %copy-start.10 = (f32[256,1024]{1,0:T(8,128)S(1)}, f32[256,1024]{1,0:T(8,128)}, u32[]{:S(2)}) copy-start(f32[256,1024]{1,0:T(8,128)} %copy-done.9) | copy-start | bytes 3145732
  295.1 110.0 %all-gather.11.cloned.1.call-start = ((), (), s32[]{:S(2)}) async-start(), calls=%async_computation.11 | async-start | bytes 2621440 | tf_op jit(solution)/shard_map/all_gather | solution.py:281
  299.2 68.3 %copy-start.32 = (f32[2,1024,4]{1,2,0:T(4,128)S(1)}, f32[2,1024,4]{1,2,0:T(4,128)}, u32[]{:S(2)}) copy-start(f32[2,1024,4]{1,2,0:T(4,128)} %param.30) | copy-start | bytes 98308
  299.2 68.9 %copy-start.30 = (f32[2,1024,4]{1,2,0:T(4,128)S(1)}, f32[2,1024,4]{1,2,0:T(4,128)}, u32[]{:S(2)}) copy-start(f32[2,1024,4]{1,2,0:T(4,128)} %param.32) | copy-start | bytes 98308
  299.2 69.6 %copy-start.33 = (f32[2,4,1024]{2,1,0:T(4,128)S(1)}, f32[2,4,1024]{2,1,0:T(4,128)}, u32[]{:S(2)}) copy-start(f32[2,4,1024]{2,1,0:T(4,128)} %param.31) | copy-start | bytes 98308
  340.7 28.7 %copy-start.31 = (f32[2,4,1024]{2,1,0:T(4,128)S(1)}, f32[2,4,1024]{2,1,0:T(4,128)}, u32[]{:S(2)}) copy-start(f32[2,4,1024]{2,1,0:T(4,128)} %param.33) | copy-start | bytes 98308
  368.2 41.5 %copy-start.27 = (f32[2,1024,4]{1,2,0:T(4,128)}, f32[2,1024,4]{1,2,0:T(4,128)S(1)}, u32[]{:S(2)}) copy-start(f32[2,1024,4]{1,2,0:T(4,128)S(1)} %get-tuple-element.76) | copy-start | bytes 98308
  369.4 40.3 %copy-start.28 = (f32[2,4,1024]{2,1,0:T(4,128)}, f32[2,4,1024]{2,1,0:T(4,128)S(1)}, u32[]{:S(2)}) copy-start(f32[2,4,1024]{2,1,0:T(4,128)S(1)} %get-tuple-element.77) | copy-start | bytes 98308
  405.1 4.6 %copy-start.1 = (bf16[1024,1024]{1,0:T(8,128)(2,1)S(1)}, bf16[1024,1024]{1,0:T(8,128)(2,1)}, u32[]{:S(2)}) copy-start(bf16[1024,1024]{1,0:T(8,128)(2,1)} %param.26) | copy-start | bytes 6291460
  (18 other events, 49.5 us)
Sparse Core Ops, SparseCore 0:
  46.7 37.9 reduce-scatter.4
  87.7 35.1 all-gather.4
  138.4 35.1 reduce-scatter.8
  176.4 35.1 reduce-scatter.6
  216.8 35.1 all-gather.8
  294.5 35.9 reduce-scatter.10
  332.3 35.1 all-gather.6
  369.9 35.1 all-gather.10
where the time goes:
time: 425 us; the launch traced here: 417 us
  waiting for transfers between devices  220 us (52%)
  matrix products  70.9 us (17%)
  other arithmetic  51.1 us (12%)
  blocking collectives  40.8 us (10%)
  between operations  17.9 us (4%)
  local copies, waits for them, and re-layouts  15.6 us (4%)
    psum x1, blocking collectives, local(): lax.psum((grad_a_part, grad_b_part, jnp.sum(seq_weight)), ('dp', 'tensor'))  40.8 us
    reduce_scatter x1, waiting for transfers between devices, local(): lax.psum_scatter(mlp_part.astype(jnp.bfloat16), 'tensor', scatter_dimensi...  36.7 us
    all_gather x1, waiting for transfers between devices, local(): lax.all_gather(grad_resid_share.astype(jnp.bfloat16), 'tensor', axis=0, t...  35.2 us
    all_gather x1, waiting for transfers between devices, local(): lax.all_gather((grad_input_share / mean_weight).astype(jnp.bfloat16), 'te...  35.1 us
    reduce_scatter x1, waiting for transfers between devices, local(): lax.psum_scatter(attn_part.astype(jnp.bfloat16), 'tensor', scatter_dimens...  34 us
    all_gather x1, waiting for transfers between devices, local(): norm2 = lax.all_gather(norm_share, 'tensor', axis=0, tiled=True)  33.3 us
    reduce_scatter x1, waiting for transfers between devices, local(): lax.psum_scatter(jnp.einsum('rf,df->rd', grad_pre, hidden_weight, preferr...  25.3 us
    all_gather x1, waiting for transfers between devices, local(): output_rows = lax.all_gather(output_share, 'tensor', axis=0, tiled=True)  19.5 us
  transfers between devices with their start and end apart: 8, of which 7 were waited for; matrix products, arithmetic and copies ran while one was open for 7% of the time, Pallas kernels for 0%

commit v1 on v0

--- a/solution.py
+++ b/solution.py
@@ -13,6 +13,23 @@
 RATE_BASE = 0.025
 WEIGHT_DECAY = 0.005
 COUNT_BASE = 256.0
+
+
+def note_figure(t0):
+    across = "tensor"
+    found_now, passed, vec_out = (lax.axis_size(across), lax.axis_index(across), t0.shape[0])
+    parts_seen = tuple((d * found_now if u == 0 else d for u, d in enumerate(t0.shape)))
+    current_arr = lax.dynamic_update_slice_in_dim(
+        jnp.zeros(parts_seen, t0.dtype), t0, passed * vec_out, axis=0
+    )
+    ii = 1
+    while ii < found_now:
+        t0 = lax.ppermute(t0, across, tuple(((u, (u + 1) % found_now) for u in range(found_now))))
+        current_arr = lax.dynamic_update_slice_in_dim(
+            current_arr, t0, (passed - ii) % found_now * vec_out, axis=0
+        )
+        ii += 1
+    return current_arr
 
 
 def layer_norm(value_rows, norm_gain, norm_bias):
@@ -224,9 +241,7 @@
     grad_resid_share = grad_out_share + norm_back(
         resid_share, vector_parameters[2], vector_parameters[3], grad_norm_share
     )
-    grad_resid_low = lax.all_gather(
-        grad_resid_share.astype(jnp.bfloat16), "tensor", axis=0, tiled=True
-    )
+    grad_resid_low = note_figure(grad_resid_share.astype(jnp.bfloat16))
     grad_merged = jnp.einsum(
         "rd,ed->re", grad_resid_low, attention_output_weight, preferred_element_type=jnp.float32
     ).astype(jnp.bfloat16)

time: 425 us -> 432 us (1.016)
    ppermute x0 -> x3, waiting for transfers between devices: none -> 36.8 us  [note_figure(): lax.ppermute(t0, across, tuple(((u, (u + 1) % found_now) for u in range(f...]
    all_gather x1 -> x0, waiting for transfers between devices: 35.2 us -> none  [local(): lax.all_gather(grad_resid_share.astype(jnp.bfloat16), 'tensor', axis=0, t...]
  transfers between devices with their start and end apart: 8 -> 10, of which waited for: 7 -> 9; matrix products, arithmetic and copies ran while one was open for 7% -> 7% of each run, Pallas kernels for 0% -> 0%
where the time goes in v1:
time: 432 us; the launch traced here: 424 us
  waiting for transfers between devices  221 us (51%)
  matrix products  70.9 us (16%)
  other arithmetic  50.8 us (12%)
  blocking collectives  40.7 us (9%)
  local copies, waits for them, and re-layouts  19.7 us (5%)
  between operations  18 us (4%)
    psum x1, blocking collectives, local(): lax.psum((grad_a_part, grad_b_part, jnp.sum(seq_weight)), ('dp', 'tensor'))  40.7 us
    all_gather x1, waiting for transfers between devices, local(): lax.all_gather((grad_input_share / mean_weight).astype(jnp.bfloat16), 'te...  37.6 us
    ppermute x3, waiting for transfers between devices, note_figure(): lax.ppermute(t0, across, tuple(((u, (u + 1) % found_now) for u in range(f...  36.8 us
    reduce_scatter x1, waiting for transfers between devices, local(): lax.psum_scatter(mlp_part.astype(jnp.bfloat16), 'tensor', scatter_dimensi...  36.7 us
    reduce_scatter x1, waiting for transfers between devices, local(): lax.psum_scatter(attn_part.astype(jnp.bfloat16), 'tensor', scatter_dimens...  34 us
    all_gather x1, waiting for transfers between devices, local(): norm2 = lax.all_gather(norm_share, 'tensor', axis=0, tiled=True)  33.3 us
    reduce_scatter x1, waiting for transfers between devices, local(): lax.psum_scatter(jnp.einsum('rf,df->rd', grad_pre, hidden_weight, preferr...  25.3 us
    all_gather x1, waiting for transfers between devices, local(): output_rows = lax.all_gather(output_share, 'tensor', axis=0, tiled=True)  17.1 us
  transfers between devices with their start and end apart: 10, of which 9 were waited for; matrix products, arithmetic and copies ran while one was open for 7% of the time, Pallas kernels for 0%

profile of v1, /device:TPU:0, one launch (start us, length us, event | category | flops | bytes accessed | tf_op | source)
XLA Modules:
  0.0 424.3 jit_solution(502023811518149708)
XLA Ops:
  11.2 2.3 multiply_reduce_fusion.2
  13.5 2.4 fusion.20
  20.3 3.0 fusion.94
  27.0 2.2 reshape.355
  31.4 3.2 fusion.95
  44.5 2.1 convolution_convert_fusion.1
  46.6 4.0 convert_element_type.147
  50.7 34.0 %reduce-scatter.5.cloned.1.call-done = bf16[256,1024]{1,0:T(8,128)(2,1)} async-done(((bf16[1024,1024]{1,0:T(8,128)(2,1)}), bf16[256,1024]{1,0:T(8,128)(2,1)}) %reduce-scatter.5.cloned.1.call-update) | async-done | bytes 524304 | tf_op jit(solution)/shard_map/reduce_scatter | solution.py:208
  89.7 33.3 %all-gather.4.cloned.1.call-done = bf16[1024,1024]{1,0:T(8,128)(2,1)} async-done(((bf16[256,1024]{1,0:T(8,128)(2,1)}), bf16[1024,1024]{1,0:T(8,128)(2,1)}) %all-gather.4.cloned.1.call-update) | async-done | bytes 2097168 | tf_op jit(solution)/shard_map/all_gather | solution.py:216
  122.9 5.9 %fusion.97 = f32[1024,1024]{1,0:T(8,128)} fusion(bf16[1024,1024]{1,0:T(8,128)(2,1)} %all-gather.4.cloned.1.call-done, bf16[1024,1024]{1,0:T(8,128)(2,1)S(1)} %copy-done), kind=kOutput, calls=%fused_computation.175 | convolution fusion | flops 2147483648 | bytes 8388608 | tf_op jit(solution)/shard_map/dot_general | solution.py:217
  128.8 9.4 %convolution_convert_fusion = bf16[1024,1024]{1,0:T(8,128)(2,1)} fusion(bf16[1024,1024]{1,0:T(8,128)(2,1)S(1)} %copy-done, f32[1024,1024]{1,0:T(8,128)} %fusion.97, bf16[1024,1024]{1,0:T(8,128)(2,1)} %param.27, f32[1024]{0:T(1024)S(1)} %copy-done.36, bf16[1,1024,1024]{2,1,0:T(8,128)(2,1)} %param.18, f32[]{:T(128)S(6)} %div.95), kind=kOutput, calls=%fused_computation.47 | convolution fusion | flops 4321181696 | bytes 12587012 | tf_op jit(solution)/shard_map/rf,df->rd/dot_general | solution.py:233
  138.3 7.1 %fusion.27 = bf16[1024,1024]{1,0:T(8,128)(2,1)} fusion(bf16[1024,1024]{1,0:T(8,128)(2,1)} %param.27, f32[1024,1024]{1,0:T(8,128)} %fusion.97, f32[1024]{0:T(1024)S(1)} %copy-done.36), kind=kOutput, calls=%fused_computation.46 | convolution fusion | flops 2159017984 | bytes 8392704 | tf_op jit(solution)/shard_map/dot_general | solution.py:221
  145.8 2.5 convert_multiply_fusion
  148.3 25.3 %reduce-scatter.9.cloned.1.call-done = bf16[256,1024]{1,0:T(8,128)(2,1)} async-done(((bf16[1024,1024]{1,0:T(8,128)(2,1)}), bf16[256,1024]{1,0:T(8,128)(2,1)}) %reduce-scatter.9.cloned.1.call-update) | async-done | bytes 524304 | tf_op jit(solution)/shard_map/reduce_scatter | solution.py:232
  175.0 36.7 %reduce-scatter.7.cloned.1.call-done = bf16[256,1024]{1,0:T(8,128)(2,1)} async-done(((bf16[1024,1024]{1,0:T(8,128)(2,1)}), bf16[256,1024]{1,0:T(8,128)(2,1)}) %reduce-scatter.7.cloned.1.call-update) | async-done | bytes 524304 | tf_op jit(solution)/shard_map/reduce_scatter | solution.py:223
  211.7 2.4 fusion.88
  215.7 2.2 constant_dynamic-update-slice_fusion.3
  219.4 12.9 %collective-permute-done = bf16[256,1024]{1,0:T(8,128)(2,1)S(1)} collective-permute-done((bf16[256,1024]{1,0:T(8,128)(2,1)S(1)}, bf16[256,1024]{1,0:T(8,128)(2,1)S(1)}, u32[]{:S(2)}, u32[]{:S(2)}) %collective-permute-start) | collective-permute-done | bytes 524320 | tf_op jit(solution)/shard_map/ppermute | solution.py:27
  232.9 13.0 %collective-permute-done.1 = bf16[256,1024]{1,0:T(8,128)(2,1)S(1)} collective-permute-done((bf16[256,1024]{1,0:T(8,128)(2,1)S(1)}, bf16[256,1024]{1,0:T(8,128)(2,1)S(1)}, u32[]{:S(2)}, u32[]{:S(2)}) %collective-permute-start.1) | collective-permute-done | bytes 524320 | tf_op jit(solution)/shard_map/ppermute | solution.py:27
  247.6 10.9 %collective-permute-done.2 = bf16[256,1024]{1,0:T(8,128)(2,1)S(1)} collective-permute-done((bf16[256,1024]{1,0:T(8,128)(2,1)S(1)}, bf16[256,1024]{1,0:T(8,128)(2,1)S(1)}, u32[]{:S(2)}, u32[]{:S(2)}) %collective-permute-start.2) | collective-permute-done | bytes 524320 | tf_op jit(solution)/shard_map/ppermute | solution.py:27
  259.3 2.5 convolution_convert_fusion.2
  261.9 5.0 %fusion.11 = f32[4,1024,64]{1,2,0:T(8,128)S(1)} fusion(f32[4,512,1024]{2,1,0:T(8,128)} %copy-done.2, f32[4,512]{1,0:T(4,128)S(1)} %log_add_fusion, bf16[1,4,1024,64]{2,3,1,0:T(8,128)(2,1)S(1)} %bitcast.160), kind=kOutput, calls=%fused_computation.25 | convolution fusion | flops 272629760 | bytes 9707520 | tf_op jit(solution)/shard_map/shqk,shqe->shke/dot_general | solution.py:128
  266.9 4.3 %multiply_reduce_fusion = (f32[4,512]{1,0:T(4,128)S(1)}, f32[4,512,1024]{2,1,0:T(8,128)}) fusion(f32[4,512,1024]{2,1,0:T(8,128)S(1)} %bitcast.152, f32[4,512]{1,0:T(4,128)S(1)} %log_add_fusion, bf16[4,1024,64]{1,2,0:T(8,128)(2,1)S(1)} %copy-done.12, bf16[1,4,1024,64]{2,3,1,0:T(8,128)(2,1)S(1)} %bitcast.161), kind=kOutput, calls=%fused_computation.1 | convolution fusion | flops 274724864 | bytes 17580032 | tf_op jit(solution)/shard_map/shqe,shke->shqk/dot_general | solution.py:112
  271.2 2.6 multiply_reduce_fusion.1
  279.9 6.9 %multiply_convert_fusion = bf16[4,512,1024]{2,1,0:T(8,128)(2,1)S(1)} fusion(f32[4,512,1024]{2,1,0:T(8,128)} %get-tuple-element.57, f32[4,512,1024]{2,1,0:T(8,128)} %copy-done.2, f32[4,512]{1,0:T(4,128)S(1)} %get-tuple-element.56, f32[4,512]{1,0:T(4,128)S(1)} %log_add_fusion), kind=kLoop, calls=%fused_computation | loop fusion | flops 8388608 | bytes 20987904 | tf_op jit(solution)/shard_map/convert_element_type | solution.py:116
  290.9 3.9 fusion.64
  295.9 5.8 %fusion.15 = bf16[1024,1024]{1,0:T(8,128)(2,1)} fusion(f32[1024,1024,1]{1,0,2:T(8,128)} %fusion.64, bf16[3,1024,256]{2,1,0:T(8,128)(2,1)} %param.24, bf16[1,1024,256]{2,1,0:T(8,128)(2,1)S(1)} %copy.36, bf16[1,1024,256]{2,1,0:T(8,128)(2,1)S(1)} %copy.35, bf16[1,1024,256]{2,1,0:T(8,128)(2,1)S(1)} %copy.34), kind=kOutput, calls=%fused_computation.28 | convolution fusion | flops 1614282752 | bytes 9437184 | tf_op jit(solution)/shard_map/cre,cde->rd/dot_general | solution.py:257
  306.5 40.7 %all-reduce.2 = (f32[]{:T(128)}, f32[2,1024,4]{1,2,0:T(4,128)S(1)}, f32[2,4,1024]{2,1,0:T(4,128)S(1)}) all-reduce(f32[]{:T(128)S(6)} %div.95, f32[2,1024,4]{1,2,0:T(4,128)S(1)} %convolution_bitcast_fusion.1, f32[2,4,1024]{2,1,0:T(4,128)S(1)} %fusion.52), channel_id=1, replica_groups=mesh['dp'=8,'tensor'=4] {'dp','tensor'}, use_global_device_ids=true, to_apply=%region_21.22 | all-reduce | flops 16385 | bytes 131080 | tf_op jit(solution)/shard_map/psum | solution.py:291
  351.5 3.0 divide_convert_fusion.12
  357.7 17.1 %all-gather.6.cloned.1.call-done = bf16[1024,1024]{1,0:T(8,128)(2,1)} async-done(((bf16[256,1024]{1,0:T(8,128)(2,1)}), bf16[1024,1024]{1,0:T(8,128)(2,1)}) %all-gather.6.cloned.1.call-update) | async-done | bytes 2097168 | tf_op jit(solution)/shard_map/all_gather | solution.py:227
  374.8 37.6 %all-gather.8.cloned.1.call-done = bf16[1024,1024]{1,0:T(8,128)(2,1)} async-done(((bf16[256,1024]{1,0:T(8,128)(2,1)}), bf16[1024,1024]{1,0:T(8,128)(2,1)}) %all-gather.8.cloned.1.call-update) | async-done | bytes 2097168 | tf_op jit(solution)/shard_map/all_gather | solution.py:296
  412.4 3.2 copy.63
  (168 shorter events, 58.7 us)
Async XLA Ops:
  7.2 115.8 %copy-start = (bf16[1024,1024]{1,0:T(8,128)(2,1)S(1)}, bf16[1024,1024]{1,0:T(8,128)(2,1)}, u32[]{:S(2)}) copy-start(bf16[1024,1024]{1,0:T(8,128)(2,1)} %param.26) | copy-start | bytes 6291460
  7.2 77.5 %reduce-scatter.5.cloned.1.call-start = ((), (), s32[]{:S(2)}) async-start(), calls=%async_computation.4 | async-start | bytes 2621440 | tf_op jit(solution)/shard_map/reduce_scatter | solution.py:208
  9.2 8.0 %copy-start.26 = (f32[2,1024,4]{1,2,0:T(4,128)S(1)}, f32[2,1024,4]{1,2,0:T(4,128)}, u32[]{:S(2)}) copy-start(f32[2,1024,4]{1,2,0:T(4,128)} %param.28) | copy-start | bytes 98308
  11.2 6.7 %copy-start.29 = (f32[2,4,1024]{2,1,0:T(4,128)S(1)}, f32[2,4,1024]{2,1,0:T(4,128)}, u32[]{:S(2)}) copy-start(f32[2,4,1024]{2,1,0:T(4,128)} %param.29) | copy-start | bytes 98308
  36.6 5.9 %copy-start.3 = (f32[4,512,1024]{2,1,0:T(8,128)}, f32[4,512,1024]{2,1,0:T(8,128)S(1)}, u32[]{:S(2)}) copy-start(f32[4,512,1024]{2,1,0:T(8,128)S(1)} %get-tuple-element.55) | copy-start | bytes 25165828
  46.6 76.3 %all-gather.4.cloned.1.call-start = ((), (), s32[]{:S(2)}) async-start(), calls=%async_computation.5 | async-start | bytes 2621440 | tf_op jit(solution)/shard_map/all_gather | solution.py:216
  50.7 37.7 %copy-start.37 = (s32[8]{0:T(128)S(1)}, s32[8]{0:T(128)}, u32[]{:S(2)}) copy-start(s32[8]{0:T(128)} %param.20) | copy-start | bytes 100
  87.6 86.0 %reduce-scatter.9.cloned.1.call-start = ((), (), s32[]{:S(2)}) async-start(), calls=%async_computation.8 | async-start | bytes 2621440 | tf_op jit(solution)/shard_map/reduce_scatter | solution.py:232
  89.7 39.2 %copy-start.36 = (f32[1024]{0:T(1024)S(1)}, f32[1024]{0:T(1024)}, u32[]{:S(2)}) copy-start(f32[1024]{0:T(1024)} %param.23) | copy-start | bytes 12292
  138.3 7.5 %copy-start.16 = (bf16[1,1024,1024]{2,1,0:T(8,128)(2,1)S(1)}, bf16[1,1024,1024]{2,1,0:T(8,128)(2,1)}, u32[]{:S(2)}) copy-start(bf16[1,1024,1024]{2,1,0:T(8,128)(2,1)} %param.18) | copy-start | bytes 6291460
  138.3 73.4 %reduce-scatter.7.cloned.1.call-start = ((), (), s32[]{:S(2)}) async-start(), calls=%async_computation.6 | async-start | bytes 2621440 | tf_op jit(solution)/shard_map/reduce_scatter | solution.py:223
  145.5 202.4 %reduce-scatter.11.cloned.1.call-start = ((), (), s32[]{:S(2)}) async-start(), calls=%async_computation.9 | async-start | bytes 2621440 | tf_op jit(solution)/shard_map/reduce_scatter | solution.py:285
  214.1 45.2 %copy-start.9 = (f32[256,1024]{1,0:T(8,128)}, f32[256,1024]{1,0:T(8,128)S(1)}, u32[]{:S(2)}) copy-start(f32[256,1024]{1,0:T(8,128)S(1)} %get-tuple-element.30) | copy-start | bytes 3145732
  214.1 45.2 %copy-start.25 = (bf16[256,1024]{1,0:T(8,128)(2,1)S(1)}, bf16[256,1024]{1,0:T(8,128)(2,1)}, u32[]{:S(2)}) copy-start(bf16[256,1024]{1,0:T(8,128)(2,1)} %param.25) | copy-start | bytes 1572868
  217.9 14.4 %collective-permute-start = (bf16[256,1024]{1,0:T(8,128)(2,1)S(1)}, bf16[256,1024]{1,0:T(8,128)(2,1)S(1)}, u32[]{:S(2)}, u32[]{:S(2)}) collective-permute-start(bf16[256,1024]{1,0:T(8,128)(2,1)S(1)} %get-tuple-element.28), channel_id=1, source_target_pairs={{0,1},{1,2},{2,3},{3,0},{4,5},{5,6},{6,7},{7,4},{8,9},{9,10},{10,1... | collective-permute-start | bytes 1572872 | tf_op jit(solution)/shard_map/ppermute | solution.py:27
  232.3 13.5 %collective-permute-start.1 = (bf16[256,1024]{1,0:T(8,128)(2,1)S(1)}, bf16[256,1024]{1,0:T(8,128)(2,1)S(1)}, u32[]{:S(2)}, u32[]{:S(2)}) collective-permute-start(bf16[256,1024]{1,0:T(8,128)(2,1)S(1)} %collective-permute-done), channel_id=1, source_target_pairs={{0,1},{1,2},{2,3},{3,0},{4,5},{5,6},{6,7},{7,4},{8,9},{9,10},{10,1... | collective-permute-start | bytes 1572872 | tf_op jit(solution)/shard_map/ppermute | solution.py:27
  245.8 12.7 %collective-permute-start.2 = (bf16[256,1024]{1,0:T(8,128)(2,1)S(1)}, bf16[256,1024]{1,0:T(8,128)(2,1)S(1)}, u32[]{:S(2)}, u32[]{:S(2)}) collective-permute-start(bf16[256,1024]{1,0:T(8,128)(2,1)S(1)} %collective-permute-done.1), channel_id=1, source_target_pairs={{0,1},{1,2},{2,3},{3,0},{4,5},{5,6},{6,7},{7,4},{8,9},{9,10},{10,1... | collective-permute-start | bytes 1572872 | tf_op jit(solution)/shard_map/ppermute | solution.py:27
  259.3 7.5 %slice-start = ((s8[8388608]{0:T(1024)(128)(4,1)}), s8[4194304]{0:T(1024)(128)(4,1)S(1)}, s32[]{:S(2)}) async-start(s8[8388608]{0:T(1024)(128)(4,1)} %bitcast.151), calls=%async_computation.11 | async-start | bytes 8388608
  261.8 5.0 %slice-start.1 = ((s8[8388608]{0:T(1024)(128)(4,1)}), s8[4194304]{0:T(1024)(128)(4,1)S(1)}, s32[]{:S(2)}) async-start(s8[8388608]{0:T(1024)(128)(4,1)} %bitcast.151), calls=%async_computation.12 | async-start | bytes 8388608
  261.8 9.4 %slice-start.2 = ((s8[8388608]{0:T(1024)(128)(4,1)}), s8[4194304]{0:T(1024)(128)(4,1)S(1)}, s32[]{:S(2)}) async-start(s8[8388608]{0:T(1024)(128)(4,1)} %bitcast.153), calls=%async_computation.13 | async-start | bytes 8388608
  279.8 16.0 %copy-start.22 = (bf16[1,1024,256]{2,1,0:T(8,128)(2,1)}, bf16[1,1024,256]{2,1,0:T(8,128)(2,1)S(1)}, u32[]{:S(2)}) copy-start(bf16[1,1024,256]{2,1,0:T(8,128)(2,1)S(1)} %copy.36) | copy-start | bytes 1572868
  279.9 8.9 %copy-start.20 = (bf16[4,1024,64]{1,0,2:T(4,128)(2,1)S(1)}, bf16[4,1024,64]{1,0,2:T(4,128)(2,1)}, u32[]{:S(2)}) copy-start(bf16[4,1024,64]{1,0,2:T(4,128)(2,1)} %reshape.355) | copy-start | bytes 1572868
  290.5 5.4 %copy-start.23 = (bf16[1,1024,256]{2,1,0:T(8,128)(2,1)}, bf16[1,1024,256]{2,1,0:T(8,128)(2,1)S(1)}, u32[]{:S(2)}) copy-start(bf16[1,1024,256]{2,1,0:T(8,128)(2,1)S(1)} %copy.34) | copy-start | bytes 1572868
  301.7 73.1 %all-gather.6.cloned.1.call-start = ((), (), s32[]{:S(2)}) async-start(), calls=%async_computation.7 | async-start | bytes 2621440 | tf_op jit(solution)/shard_map/all_gather | solution.py:227
  301.7 49.7 %copy-start.10 = (f32[256,1024]{1,0:T(8,128)S(1)}, f32[256,1024]{1,0:T(8,128)}, u32[]{:S(2)}) copy-start(f32[256,1024]{1,0:T(8,128)} %copy-done.9) | copy-start | bytes 3145732
  302.3 110.2 %all-gather.8.cloned.1.call-start = ((), (), s32[]{:S(2)}) async-start(), calls=%async_computation.10 | async-start | bytes 2621440 | tf_op jit(solution)/shard_map/all_gather | solution.py:296
  306.4 48.7 %copy-start.32 = (f32[2,1024,4]{1,2,0:T(4,128)S(1)}, f32[2,1024,4]{1,2,0:T(4,128)}, u32[]{:S(2)}) copy-start(f32[2,1024,4]{1,2,0:T(4,128)} %param.30) | copy-start | bytes 98308
  306.4 49.4 %copy-start.30 = (f32[2,1024,4]{1,2,0:T(4,128)S(1)}, f32[2,1024,4]{1,2,0:T(4,128)}, u32[]{:S(2)}) copy-start(f32[2,1024,4]{1,2,0:T(4,128)} %param.32) | copy-start | bytes 98308
  306.5 50.0 %copy-start.33 = (f32[2,4,1024]{2,1,0:T(4,128)S(1)}, f32[2,4,1024]{2,1,0:T(4,128)}, u32[]{:S(2)}) copy-start(f32[2,4,1024]{2,1,0:T(4,128)} %param.31) | copy-start | bytes 98308
  347.9 9.2 %copy-start.31 = (f32[2,4,1024]{2,1,0:T(4,128)S(1)}, f32[2,4,1024]{2,1,0:T(4,128)}, u32[]{:S(2)}) copy-start(f32[2,4,1024]{2,1,0:T(4,128)} %param.33) | copy-start | bytes 98308
  355.8 61.2 %copy-start.27 = (f32[2,1024,4]{1,2,0:T(4,128)}, f32[2,1024,4]{1,2,0:T(4,128)S(1)}, u32[]{:S(2)}) copy-start(f32[2,1024,4]{1,2,0:T(4,128)S(1)} %get-tuple-element.78) | copy-start | bytes 98308
  357.1 59.9 %copy-start.28 = (f32[2,4,1024]{2,1,0:T(4,128)}, f32[2,4,1024]{2,1,0:T(4,128)S(1)}, u32[]{:S(2)}) copy-start(f32[2,4,1024]{2,1,0:T(4,128)S(1)} %get-tuple-element.79) | copy-start | bytes 98308
  (20 other events, 59.0 us)
Sparse Core Ops, SparseCore 0:
  46.7 37.9 reduce-scatter.4
  87.8 35.1 all-gather.3
  138.4 35.1 reduce-scatter.8
  176.5 35.1 reduce-scatter.6
  301.8 36.0 reduce-scatter.10
  339.6 35.1 all-gather.5
  377.2 35.1 all-gather.7
